TPU v7x, 32 devices: a whole 2x2x4 slice. The times are simulated.
32 devices in a mesh: dp: 8 (over z, y), tensor: 4 (over x, core).
Axes of the slice: x: 2, y: 2, z: 4, core: 2. Of those that a mesh axis runs over, the one named last changes fastest.
Arguments:
- block_in: bfloat16 [16384, 768], P(('dp', 'tensor')), may hold values from -6 to 6
- enc_states: bfloat16 [65536, 768], P(('dp', 'tensor')), may hold values from -6 to 6
- dec_len: int32 [64], P('dp'), may hold values from 32 to 256
- enc_len: int32 [64], P('dp'), may hold values from 128 to 1024
- gain_self: bfloat16 [768], replicated, may hold values from 0.5 to 1.5
- self_query: bfloat16 [768, 768], P(None, 'tensor'), may hold values from -0.02734375 to 0.02734375
- self_key: bfloat16 [768, 768], P(None, 'tensor'), may hold values from -0.21875 to 0.21875
- self_value: bfloat16 [768, 768], P(None, 'tensor'), may hold values from -0.21875 to 0.21875
- self_out: bfloat16 [768, 768], P('tensor'), may hold values from -0.875 to 0.875
- rel_table: bfloat16 [32, 12], P(None, 'tensor'), may hold values from -4 to 4
- gain_cross: bfloat16 [768], replicated, may hold values from 0.5 to 1.5
- cross_query: bfloat16 [768, 768], P(None, 'tensor'), may hold values from -0.02734375 to 0.02734375
- cross_key: bfloat16 [768, 768], P(None, 'tensor'), may hold values from -0.21875 to 0.21875
- cross_value: bfloat16 [768, 768], P(None, 'tensor'), may hold values from -0.21875 to 0.21875
- cross_out: bfloat16 [768, 768], P('tensor'), may hold values from -0.875 to 0.875
- gain_ff: bfloat16 [768], replicated, may hold values from 0.5 to 1.5
- ff_in: bfloat16 [768, 3072], P(None, 'tensor'), may hold values from -0.21875 to 0.21875
- ff_out: bfloat16 [3072, 768], P('tensor'), may hold values from -0.109375 to 0.109375
- out_grad: bfloat16 [16384, 768], P(('dp', 'tensor')), may hold values from -6 to 6
Outputs:
- block_out: bfloat16 [16384, 768], P(('dp', 'tensor'))
- grad_in: float32 [16384, 768], P(('dp', 'tensor'))
- grad_enc: float32 [65536, 768], P(('dp', 'tensor'))
- grad_gain_self: float32 [768], replicated
- grad_self_query: float32 [768, 768], P(None, 'tensor')
- grad_self_key: float32 [768, 768], P(None, 'tensor')
- grad_self_value: float32 [768, 768], P(None, 'tensor')
- grad_self_out: float32 [768, 768], P('tensor')
- grad_rel_table: float32 [32, 12], P(None, 'tensor')
- grad_gain_cross: float32 [768], replicated
- grad_cross_query: float32 [768, 768], P(None, 'tensor')
- grad_cross_key: float32 [768, 768], P(None, 'tensor')
- grad_cross_value: float32 [768, 768], P(None, 'tensor')
- grad_cross_out: float32 [768, 768], P('tensor')
- grad_gain_ff: float32 [768], replicated
- grad_ff_in: float32 [768, 3072], P(None, 'tensor')
- grad_ff_out: float32 [3072, 768], P('tensor')
All inputs are finite; a program needn't handle non-finite values.
Results may differ from a plain program's by a relative error of at most 0.025.
Values may be sent and summed in bfloat16 or wider, within the bound.
No kernel may reach another device: no remote copies, remote signals or barrier semaphores. Data moves between devices by JAX's collectives and lax.ppermute only.
A program may use at most 256 MiB of HBM per device.

v0:
```python
import math
import jax
import jax.numpy as jnp
import numpy as np
from jax import lax
from jax.sharding import PartitionSpec as P

BUCKETS = 32
MAX_DIST = 128
LEN = 256
ENC = 1024
norm_eps = 1e-06
masked_score = -1000000000.0


def bucket_limits():
    half_count = BUCKETS // 2
    growth_ratio = MAX_DIST / half_count
    return np.array(
        [
            int(math.ceil(half_count * growth_ratio ** (level_index / half_count)))
            for level_index in range(1, half_count)
        ],
        dtype=np.int32,
    )


def bucket_onehot(length):
    places = jnp.arange(length, dtype=jnp.int32)
    distance = jnp.maximum(places[:, None] - places[None, :], 0)
    limits = jnp.asarray(bucket_limits())
    above_count = jnp.sum((distance[:, :, None] >= limits[None, None, :]).astype(jnp.int32), axis=2)
    half_count = BUCKETS // 2
    buckets = jnp.where(distance < half_count, distance, half_count + above_count)
    return (buckets[:, :, None] == jnp.arange(BUCKETS, dtype=jnp.int32)[None, None, :]).astype(
        jnp.float32
    )


def collect_rows(values):
    return lax.all_gather(values, "tensor", axis=0, tiled=True)


def spread_rows(values):
    return lax.psum_scatter(values, "tensor", scatter_dimension=0, tiled=True)


def rms_norm(values, scales):
    return values * lax.rsqrt(jnp.mean(values * values, axis=-1, keepdims=True) + norm_eps) * scales


def norm_back(values, scales, incoming):
    primal, pullback = jax.vjp(rms_norm, values, scales)
    return pullback(incoming)


def smooth_act(values):
    return jax.nn.gelu(values, approximate=True)


def act_back(values, incoming):
    primal, pullback = jax.vjp(smooth_act, values)
    return pullback(incoming)[0]


def matmul(former, latter):
    return jnp.dot(former, latter, preferred_element_type=jnp.float32)


def inner_rows(former, latter):
    return lax.dot_general(
        former, latter, (((0,), (0,)), ((), ())), preferred_element_type=jnp.float32
    )


def times_transposed(former, latter):
    return lax.dot_general(
        former, latter, (((1,), (1,)), ((), ())), preferred_element_type=jnp.float32
    )


def attend_forward(query_rows, key_rows, value_rows, extra_bias, allowed):
    scores = (
        jnp.einsum("sqhd,skhd->shqk", query_rows, key_rows, preferred_element_type=jnp.float32)
        + extra_bias
    )
    scores = jnp.where(allowed, scores, masked_score)
    top_score = jnp.max(scores, axis=-1, keepdims=True)
    weights = jnp.exp(scores - top_score)
    totals = jnp.sum(weights, axis=-1, keepdims=True)
    softmax_out = (weights / totals).astype(jnp.bfloat16)
    mixed_out = jnp.einsum(
        "shqk,skhd->sqhd", softmax_out, value_rows, preferred_element_type=jnp.float32
    ).astype(jnp.bfloat16)
    return (mixed_out, top_score + jnp.log(totals))


def attend_backward(query_rows, key_rows, value_rows, extra_bias, allowed, log_totals, grad_mixed):
    scores = (
        jnp.einsum("sqhd,skhd->shqk", query_rows, key_rows, preferred_element_type=jnp.float32)
        + extra_bias
    )
    scores = jnp.where(allowed, scores, masked_score)
    softmax_out = jnp.exp(scores - log_totals)
    grad_values = jnp.einsum(
        "shqk,sqhd->skhd",
        softmax_out.astype(jnp.bfloat16),
        grad_mixed,
        preferred_element_type=jnp.float32,
    ).astype(jnp.bfloat16)
    grad_probs = jnp.einsum(
        "sqhd,skhd->shqk", grad_mixed, value_rows, preferred_element_type=jnp.float32
    )
    row_dots = jnp.sum(grad_probs * softmax_out, axis=-1, keepdims=True)
    grad_scores = (softmax_out * (grad_probs - row_dots)).astype(jnp.bfloat16)
    grad_queries = jnp.einsum(
        "shqk,skhd->sqhd", grad_scores, key_rows, preferred_element_type=jnp.float32
    ).astype(jnp.bfloat16)
    grad_keys = jnp.einsum(
        "shqk,sqhd->skhd", grad_scores, query_rows, preferred_element_type=jnp.float32
    ).astype(jnp.bfloat16)
    return (grad_queries, grad_keys, grad_values, grad_scores)


def local(
    block_in,
    enc_states,
    dec_len,
    enc_len,
    gain_self,
    self_query,
    self_key,
    self_value,
    self_out,
    rel_table,
    gain_cross,
    cross_query,
    cross_key,
    cross_value,
    cross_out,
    gain_ff,
    ff_in,
    ff_out,
    out_grad,
):
    seq_count = dec_len.shape[0]
    local_heads = rel_table.shape[1]
    head_size = self_query.shape[1] // local_heads

    def heads_view(values, length):
        return values.reshape(seq_count, length, local_heads, head_size)

    def flat_view(values):
        return values.reshape(values.shape[0] * values.shape[1], local_heads * head_size)

    places = jnp.arange(LEN, dtype=jnp.int32)
    causal = places[None, :] <= places[:, None]
    self_allowed = causal[None, None] & (places[None, None, None, :] < dec_len[:, None, None, None])
    enc_places = jnp.arange(ENC, dtype=jnp.int32)
    cross_allowed = enc_places[None, None, None, :] < enc_len[:, None, None, None]
    onehot = bucket_onehot(LEN)
    rel_bias = jnp.einsum(
        "qkb,bh->hqk", onehot, rel_table.astype(jnp.float32), precision=lax.Precision.HIGHEST
    )[None]
    scale_self = gain_self.astype(jnp.float32)
    scale_cross = gain_cross.astype(jnp.float32)
    scale_ff = gain_ff.astype(jnp.float32)
    residual = block_in.astype(jnp.float32)
    full_self = collect_rows(rms_norm(residual, scale_self).astype(jnp.bfloat16))
    query_self = heads_view(matmul(full_self, self_query).astype(jnp.bfloat16), LEN)
    key_self = heads_view(matmul(full_self, self_key).astype(jnp.bfloat16), LEN)
    value_self = heads_view(matmul(full_self, self_value).astype(jnp.bfloat16), LEN)
    mixed_self, logsum_self = attend_forward(
        query_self, key_self, value_self, rel_bias, self_allowed
    )
    mixed_self = flat_view(mixed_self)
    after_self = residual + spread_rows(matmul(mixed_self, self_out))
    full_cross = collect_rows(rms_norm(after_self, scale_cross).astype(jnp.bfloat16))
    query_cross = heads_view(matmul(full_cross, cross_query).astype(jnp.bfloat16), LEN)
    enc_full = lax.all_gather(enc_states, "tensor", axis=0, tiled=True)
    key_flat = matmul(enc_full, cross_key).astype(jnp.bfloat16)
    value_flat = matmul(enc_full, cross_value).astype(jnp.bfloat16)
    key_cross = heads_view(key_flat, ENC)
    value_cross = heads_view(value_flat, ENC)
    mixed_cross, logsum_cross = attend_forward(
        query_cross, key_cross, value_cross, 0.0, cross_allowed
    )
    mixed_cross = flat_view(mixed_cross)
    after_cross = after_self + spread_rows(matmul(mixed_cross, cross_out))
    full_ff = collect_rows(rms_norm(after_cross, scale_ff).astype(jnp.bfloat16))
    pre_act = matmul(full_ff, ff_in)
    hidden = smooth_act(pre_act).astype(jnp.bfloat16)
    block_out = (after_cross + spread_rows(matmul(hidden, ff_out))).astype(jnp.bfloat16)
    grad_top = out_grad.astype(jnp.float32)
    full_grad_ff = collect_rows(out_grad)
    grad_ff_out = inner_rows(hidden, full_grad_ff)
    grad_pre = act_back(pre_act, times_transposed(full_grad_ff, ff_out)).astype(jnp.bfloat16)
    grad_ff_in = inner_rows(full_ff, grad_pre)
    back_values, grad_gain_ff = norm_back(
        after_cross, scale_ff, spread_rows(times_transposed(grad_pre, ff_in))
    )
    grad_after_cross = grad_top + back_values
    full_grad_cross = collect_rows(grad_after_cross.astype(jnp.bfloat16))
    grad_cross_out = inner_rows(mixed_cross, full_grad_cross)
    grad_mixed_cross = heads_view(
        times_transposed(full_grad_cross, cross_out).astype(jnp.bfloat16), LEN
    )
    grad_query, grad_key, grad_value, unused = attend_backward(
        query_cross, key_cross, value_cross, 0.0, cross_allowed, logsum_cross, grad_mixed_cross
    )
    grad_query = flat_view(grad_query)
    grad_key = flat_view(grad_key)
    grad_value = flat_view(grad_value)
    grad_cross_query = inner_rows(full_cross, grad_query)
    grad_cross_key = inner_rows(enc_full, grad_key)
    grad_cross_value = inner_rows(enc_full, grad_value)
    grad_enc = lax.psum_scatter(
        (times_transposed(grad_key, cross_key) + times_transposed(grad_value, cross_value)).astype(
            jnp.bfloat16
        ),
        "tensor",
        scatter_dimension=0,
        tiled=True,
    ).astype(jnp.float32)
    back_values, grad_gain_cross = norm_back(
        after_self, scale_cross, spread_rows(times_transposed(grad_query, cross_query))
    )
    grad_after_self = grad_after_cross + back_values
    full_grad_self = collect_rows(grad_after_self.astype(jnp.bfloat16))
    grad_self_out = inner_rows(mixed_self, full_grad_self)
    grad_mixed_self = heads_view(
        times_transposed(full_grad_self, self_out).astype(jnp.bfloat16), LEN
    )
    grad_query, grad_key, grad_value, grad_scores = attend_backward(
        query_self, key_self, value_self, rel_bias, self_allowed, logsum_self, grad_mixed_self
    )
    grad_rel_table = jnp.einsum(
        "hqk,qkb->bh",
        jnp.sum(grad_scores.astype(jnp.float32), axis=0),
        onehot,
        precision=lax.Precision.HIGHEST,
    )
    grad_query = flat_view(grad_query)
    grad_key = flat_view(grad_key)
    grad_value = flat_view(grad_value)
    grad_self_query = inner_rows(full_self, grad_query)
    grad_self_key = inner_rows(full_self, grad_key)
    grad_self_value = inner_rows(full_self, grad_value)
    grad_normed = (
        times_transposed(grad_query, self_query)
        + times_transposed(grad_key, self_key)
        + times_transposed(grad_value, self_value)
    )
    back_values, grad_gain_self = norm_back(residual, scale_self, spread_rows(grad_normed))
    grad_in = grad_after_self + back_values
    (
        grad_self_query,
        grad_self_key,
        grad_self_value,
        grad_self_out,
        grad_rel_table,
        grad_cross_query,
        grad_cross_key,
        grad_cross_value,
        grad_cross_out,
        grad_ff_in,
        grad_ff_out,
    ) = (
        lax.psum(grad_self_query.astype(jnp.bfloat16), "dp").astype(jnp.float32),
        lax.psum(grad_self_key.astype(jnp.bfloat16), "dp").astype(jnp.float32),
        lax.psum(grad_self_value.astype(jnp.bfloat16), "dp").astype(jnp.float32),
        lax.psum(grad_self_out.astype(jnp.bfloat16), "dp").astype(jnp.float32),
        lax.psum(grad_rel_table.astype(jnp.bfloat16), "dp").astype(jnp.float32),
        lax.psum(grad_cross_query.astype(jnp.bfloat16), "dp").astype(jnp.float32),
        lax.psum(grad_cross_key.astype(jnp.bfloat16), "dp").astype(jnp.float32),
        lax.psum(grad_cross_value.astype(jnp.bfloat16), "dp").astype(jnp.float32),
        lax.psum(grad_cross_out.astype(jnp.bfloat16), "dp").astype(jnp.float32),
        lax.psum(grad_ff_in.astype(jnp.bfloat16), "dp").astype(jnp.float32),
        lax.psum(grad_ff_out.astype(jnp.bfloat16), "dp").astype(jnp.float32),
    )
    grad_gain_self, grad_gain_cross, grad_gain_ff = lax.psum(
        (grad_gain_self, grad_gain_cross, grad_gain_ff), ("dp", "tensor")
    )
    return (
        block_out,
        grad_in,
        grad_enc,
        grad_gain_self,
        grad_self_query,
        grad_self_key,
        grad_self_value,
        grad_self_out,
        grad_rel_table,
        grad_gain_cross,
        grad_cross_query,
        grad_cross_key,
        grad_cross_value,
        grad_cross_out,
        grad_gain_ff,
        grad_ff_in,
        grad_ff_out,
    )


def solution(mesh):
    placed = (
        P(("dp", "tensor"), None),
        P(("dp", "tensor"), None),
        P("dp"),
        P("dp"),
        P(),
        P(None, "tensor"),
        P(None, "tensor"),
        P(None, "tensor"),
        P("tensor", None),
        P(None, "tensor"),
        P(),
        P(None, "tensor"),
        P(None, "tensor"),
        P(None, "tensor"),
        P("tensor", None),
        P(),
        P(None, "tensor"),
        P("tensor", None),
        P(("dp", "tensor"), None),
    )
    return jax.shard_map(
        local,
        mesh=mesh,
        in_specs=placed,
        out_specs=(
            P(("dp", "tensor"), None),
            P(("dp", "tensor"), None),
            P(("dp", "tensor"), None),
            P(),
            P(None, "tensor"),
            P(None, "tensor"),
            P(None, "tensor"),
            P("tensor", None),
            P(None, "tensor"),
            P(),
            P(None, "tensor"),
            P(None, "tensor"),
            P(None, "tensor"),
            P("tensor", None),
            P(),
            P(None, "tensor"),
            P("tensor", None),
        ),
        check_vma=False,
    )
```

profile of v0, /device:TPU:0, one launch (start us, length us, event | category | flops | bytes accessed | tf_op | source)
XLA Modules:
  0.0 1159.5 jit_solution(13267662903418676840)
XLA Ops:
  14.8 11.5 copy.126
  28.5 15.8 %all-gather.8.cloned.1.call-done = bf16[2048,768]{1,0:T(8,128)(2,1)} async-done(((bf16[512,768]{1,0:T(8,128)(2,1)}), bf16[2048,768]{1,0:T(8,128)(2,1)}) %all-gather.8.cloned.1.call-update) | async-done | bytes 3145744 | tf_op jit(solution)/shard_map/all_gather | solution.py:41
  57.8 3.7 fusion.89
  62.4 57.7 %reduce-scatter.8.cloned.1.call-done = f32[512,768]{1,0:T(8,128)} async-done(((f32[2048,768]{1,0:T(8,128)}), f32[512,768]{1,0:T(8,128)}) %reduce-scatter.8.cloned.1.call-update) | async-done | bytes 1572880 | tf_op jit(solution)/shard_map/reduce_scatter | solution.py:45
  123.8 80.0 %all-gather.10.cloned.1.call-done = bf16[8192,768]{1,0:T(8,128)(2,1)} async-done(((bf16[2048,768]{1,0:T(8,128)(2,1)}), bf16[8192,768]{1,0:T(8,128)(2,1)}) %all-gather.10.cloned.1.call-update) | async-done | bytes 12582928 | tf_op jit(solution)/shard_map/all_gather | solution.py:180
  203.9 8.9 convolution_convert_fusion
  212.8 4.0 copy.165
  216.8 4.4 convolution_convert_fusion.1
  221.2 3.9 copy.163
  225.1 9.4 all-gather.12.cloned.1.call-done
  238.0 11.5 select_reduce_fusion
  249.5 11.0 fusion
  260.5 18.0 %fusion.58 = bf16[8,256,3,64]{1,3,2,0:T(8,128)(2,1)S(1)} fusion(f32[8,3,256,1024]{3,2,1,0:T(8,128)} %get-tuple-element.48, f32[8,3,256]{2,1,0:T(4,128)S(1)} %fusion, f32[8,3,256]{2,1,0:T(4,128)S(1)} %get-tuple-element.47, pred[8,1024]{1,0:T(8,128)(4,1)S(1)} %iota_compare_fusion.2, bf16[8,1024,3,64]{1,0,3,2:T(8,128)(2,1)} %bitcast.180), kind=kOutput, calls=%fused_computation.96 | convolution fusion | flops 830865408 | bytes 29155328 | tf_op jit(solution)/shard_map/shqk,skhd->sqhd/dot_general | solution.py:92
  279.5 3.7 fusion.90
  284.0 57.8 %reduce-scatter.10.cloned.1.call-done = f32[512,768]{1,0:T(8,128)} async-done(((f32[2048,768]{1,0:T(8,128)}), f32[512,768]{1,0:T(8,128)}) %reduce-scatter.10.cloned.1.call-update) | async-done | bytes 1572880 | tf_op jit(solution)/shard_map/reduce_scatter | solution.py:45
  345.8 26.0 %all-gather.16.cloned.1.call-done = bf16[2048,768]{1,0:T(8,128)(2,1)} async-done(((bf16[512,768]{1,0:T(8,128)(2,1)}), bf16[2048,768]{1,0:T(8,128)(2,1)}) %all-gather.16.cloned.1.call-update) | async-done | bytes 3145744 | tf_op jit(solution)/shard_map/all_gather | solution.py:41
  371.8 7.6 fusion.91
  379.4 23.1 %all-gather.14.cloned.1.call-done = bf16[2048,768]{1,0:T(8,128)(2,1)} async-done(((bf16[512,768]{1,0:T(8,128)(2,1)}), bf16[2048,768]{1,0:T(8,128)(2,1)}) %all-gather.14.cloned.1.call-update) | async-done | bytes 3145744 | tf_op jit(solution)/shard_map/all_gather | solution.py:41
  402.5 11.8 %fusion.14 = (bf16[2048,768]{1,0:T(8,128)(2,1)S(1)}, f32[2048,768]{1,0:T(8,128)}) fusion(f32[2048,768]{1,0:T(8,128)} %fusion.91, bf16[2048,768]{1,0:T(8,128)(2,1)} %all-gather.14.cloned.1.call-done, bf16[768,768]{1,0:T(8,128)(2,1)S(1)} %copy-done), kind=kOutput, calls=%fused_computation.25 | convolution fusion | flops 2447376384 | bytes 20054016 | tf_op jit(solution)/shard_map/dot_general | solution.py:67
  415.9 4.6 fusion.92
  420.6 58.4 %reduce-scatter.14.cloned.1.call-done = f32[512,768]{1,0:T(8,128)} async-done(((f32[2048,768]{1,0:T(8,128)}), f32[512,768]{1,0:T(8,128)}) %reduce-scatter.14.cloned.1.call-update) | async-done | bytes 1572880 | tf_op jit(solution)/shard_map/reduce_scatter | solution.py:45
  485.0 28.6 %all-gather.18.cloned.1.call-done = bf16[2048,768]{1,0:T(8,128)(2,1)} async-done(((bf16[512,768]{1,0:T(8,128)(2,1)}), bf16[2048,768]{1,0:T(8,128)(2,1)}) %all-gather.18.cloned.1.call-update) | async-done | bytes 3145744 | tf_op jit(solution)/shard_map/all_gather | solution.py:41
  516.9 23.6 %multiply_reduce_fusion = (f32[8,3,256]{2,1,0:T(4,128)S(1)}, f32[8,3,256,1024]{3,2,1,0:T(8,128)}) fusion(f32[8,3,256,1024]{3,2,1,0:T(8,128)} %get-tuple-element.48, f32[8,3,256]{2,1,0:T(4,128)S(1)} %log_add_fusion.1, pred[8,1024]{1,0:T(8,128)(4,1)S(1)} %iota_compare_fusion.2, bf16[8,1024,3,64]{1,0,3,2:T(8,128)(2,1)} %bitcast.181, ...), kind=kOutput, calls=%fused_computation.2 | convolution fusion | flops 830466048 | bytes 54321152 | tf_op jit(solution)/shard_map/sqhd,skhd->shqk/dot_general | solution.py:111
  540.5 21.9 %multiply_convert_fusion = bf16[8,3,256,1024]{3,2,1,0:T(8,128)(2,1)} fusion(f32[8,3,256,1024]{3,2,1,0:T(8,128)} %get-tuple-element.52, f32[8,3,256,1024]{3,2,1,0:T(8,128)} %get-tuple-element.48, f32[8,3,256]{2,1,0:T(4,128)S(1)} %get-tuple-element.51, f32[8,3,256]{2,1,0:T(4,128)S(1)} %log_add_fusion.1, pred[8,1024]{1,0:T(8,128)(4,1)S(1)} %iota_compare_fusion.2), kind=kLoop, calls=%fused_computation.1 | loop fusion | flops 31457280 | bytes 62971904 | tf_op jit(solution)/shard_map/convert_element_type | solution.py:115
  562.4 10.4 fusion.53
  575.5 3.7 fusion.93
  579.3 10.6 fusion.85
  590.7 7.0 convolution_convert_fusion.9
  597.8 7.3 convolution_convert_fusion.8
  605.1 32.7 %reduce-scatter.16.cloned.1.call-done = f32[512,768]{1,0:T(8,128)} async-done(((f32[2048,768]{1,0:T(8,128)}), f32[512,768]{1,0:T(8,128)}) %reduce-scatter.16.cloned.1.call-update) | async-done | bytes 1572880 | tf_op jit(solution)/shard_map/reduce_scatter | solution.py:45
  640.3 58.5 %reduce-scatter.12.cloned.1.call-done = f32[512,768]{1,0:T(8,128)} async-done(((f32[2048,768]{1,0:T(8,128)}), f32[512,768]{1,0:T(8,128)}) %reduce-scatter.12.cloned.1.call-update) | async-done | bytes 1572880 | tf_op jit(solution)/shard_map/reduce_scatter | solution.py:45
  698.8 5.6 fusion.86
  704.4 11.3 convert_bitcast_fusion
  719.7 8.1 convert_bitcast_fusion.1
  736.7 3.6 fusion.62
  747.2 4.0 fusion.49
  751.2 4.4 multiply_reduce_fusion.1
  755.6 5.7 convert_reduce_fusion
  772.7 13.9 %fusion.96 = f32[8192,768]{1,0:T(8,128)} fusion(bf16[8192,192]{0,1:T(8,128)(2,1)} %bitcast.179, bf16[768,192]{0,1:T(8,128)(2,1)S(1)} %copy-done.35), kind=kOutput, calls=%fused_computation.154 | convolution fusion | flops 2415919104 | bytes 28606464 | tf_op jit(solution)/shard_map/dot_general | solution.py:77
  786.6 14.6 %add_convert_fusion = bf16[8192,768]{1,0:T(8,128)(2,1)} fusion(f32[8192,768]{1,0:T(8,128)} %fusion.96, bf16[8192,192]{0,1:T(8,128)(2,1)} %bitcast.177, bf16[768,192]{0,1:T(8,128)(2,1)S(1)} %copy-done.37), kind=kOutput, calls=%fused_computation | convolution fusion | flops 2428502016 | bytes 41189376 | tf_op jit(solution)/shard_map/dot_general | solution.py:77
  804.4 3.8 add_add_fusion
  809.4 4.1 fusion.63
  813.5 22.4 %psum.103 = bf16[32,3]{0,1:T(4,128)(2,1)S(1)} all-reduce(bf16[32,3]{0,1:T(4,128)(2,1)S(1)} %fusion.63), channel_id=1, replica_groups=mesh['dp'=8,'tensor'=4] {'dp'}, use_global_device_ids=true, to_apply=%region_27.28 | all-reduce | flops 96 | bytes 384 | tf_op jit(solution)/shard_map/psum | solution.py:273
  836.5 108.9 %all-reduce.4.cloned.1.call-done = (bf16[768,192]{0,1:T(8,128)(2,1)}, bf16[768,192]{0,1:T(8,128)(2,1)}, bf16[768,192]{0,1:T(8,128)(2,1)}, bf16[192,768]{1,0:T(8,...) async-done(((bf16[768,192]{0,1:T(8,128)(2,1)}, ...) | async-done | bytes 4718608 | tf_op jit(solution)/shard_map/psum | solution.py:269
  959.5 86.4 %reduce-scatter.20.cloned.1.call-done = bf16[2048,768]{1,0:T(8,128)(2,1)} async-done(((bf16[8192,768]{1,0:T(8,128)(2,1)}), bf16[2048,768]{1,0:T(8,128)(2,1)}) %reduce-scatter.20.cloned.1.call-update) | async-done | bytes 3145744 | tf_op jit(solution)/shard_map/reduce_scatter | solution.py:217
  1045.9 5.1 convert_element_type.260
  1050.9 55.8 %reduce-scatter.18.cloned.1.call-done = f32[512,768]{1,0:T(8,128)} async-done(((f32[2048,768]{1,0:T(8,128)}), f32[512,768]{1,0:T(8,128)}) %reduce-scatter.18.cloned.1.call-update) | async-done | bytes 1572880 | tf_op jit(solution)/shard_map/reduce_scatter | solution.py:45
  1110.1 39.7 %all-reduce = (f32[768]{0:T(1024)}, f32[768]{0:T(1024)}, f32[768]{0:T(1024)}) all-reduce(f32[768]{0:T(1024)} %get-tuple-element.21, f32[768]{0:T(1024)} %get-tuple-element.19, f32[768]{0:T(1024)S(1)} %copy-done.77), channel_id=1, replica_groups=mesh['dp'=8,'tensor'=4] {'dp','tensor'}, use_global_device_ids=true, to_apply=%region_21.22 | all-reduce | flops 2304 | bytes 18432 | tf_op jit(solution)/shard_map/psum | solution.py:281
  (303 shorter events, 109.7 us)
Async XLA Ops:
  7.2 395.3 %copy-start = (bf16[768,768]{1,0:T(8,128)(2,1)S(1)}, bf16[768,768]{1,0:T(8,128)(2,1)}, u32[]{:S(2)}) copy-start(bf16[768,768]{1,0:T(8,128)(2,1)} %param.36) | copy-start | bytes 3538948
  7.2 37.0 %all-gather.8.cloned.1.call-start = ((), (), s32[]{:S(2)}) async-start(), calls=%async_computation.7 | async-start | bytes 3932160 | tf_op jit(solution)/shard_map/all_gather | solution.py:41
  12.9 107.2 %reduce-scatter.8.cloned.1.call-start = ((), (), s32[]{:S(2)}) async-start(), calls=%async_computation.8 | async-start | bytes 7864320 | tf_op jit(solution)/shard_map/reduce_scatter | solution.py:45
  13.6 12.7 %copy-start.80 = (bf16[32,3]{0,1:T(4,128)(2,1)S(1)}, bf16[32,3]{0,1:T(4,128)(2,1)}, u32[]{:S(2)}) copy-start(bf16[32,3]{0,1:T(4,128)(2,1)} %param.29) | copy-start | bytes 580
  26.3 17.9 %copy-start.49 = (bf16[768,192]{0,1:T(8,128)(2,1)S(1)}, bf16[768,192]{0,1:T(8,128)(2,1)}, u32[]{:S(2)}) copy-start(bf16[768,192]{0,1:T(8,128)(2,1)} %param.26) | copy-start | bytes 884740
  28.4 19.2 %copy-start.47 = (bf16[768,192]{0,1:T(8,128)(2,1)S(1)}, bf16[768,192]{0,1:T(8,128)(2,1)}, u32[]{:S(2)}) copy-start(bf16[768,192]{0,1:T(8,128)(2,1)} %param.25) | copy-start | bytes 884740
  61.6 58.5 %copy-start.9 = (bf16[512,768]{1,0:T(8,128)(2,1)S(1)}, bf16[512,768]{1,0:T(8,128)(2,1)}, u32[]{:S(2)}) copy-start(bf16[512,768]{1,0:T(8,128)(2,1)} %param.20) | copy-start | bytes 2359300
  61.6 142.3 %all-gather.10.cloned.1.call-start = ((), (), s32[]{:S(2)}) async-start(), calls=%async_computation.9 | async-start | bytes 15728640 | tf_op jit(solution)/shard_map/all_gather | solution.py:180
  62.3 172.2 %all-gather.12.cloned.1.call-start = ((), (), s32[]{:S(2)}) async-start(), calls=%async_computation.10 | async-start | bytes 3932160 | tf_op jit(solution)/shard_map/all_gather | solution.py:41
  62.4 61.0 %copy-start.61 = (f32[768]{0:T(1024)}, f32[768]{0:T(1024)S(1)}, u32[]{:S(2)}) copy-start(f32[768]{0:T(1024)S(1)} %convert_element_type.226) | copy-start | bytes 9220
  62.4 61.3 %copy-start.83 = (s32[8]{0:T(128)S(1)}, s32[8]{0:T(128)}, u32[]{:S(2)}) copy-start(s32[8]{0:T(128)} %param.23) | copy-start | bytes 100
  122.4 90.4 %copy-start.67 = (f32[512]{0:T(512)}, f32[512]{0:T(512)S(1)}, u32[]{:S(2)}) copy-start(f32[512]{0:T(512)S(1)} %fusion.79) | copy-start | bytes 6148
  123.5 218.3 %reduce-scatter.10.cloned.1.call-start = ((), (), s32[]{:S(2)}) async-start(), calls=%async_computation.11 | async-start | bytes 7864320 | tf_op jit(solution)/shard_map/reduce_scatter | solution.py:45
  203.9 12.9 %copy-start.84 = (bf16[8192,768]{1,0:T(8,128)(2,1)S(1)}, bf16[8192,768]{1,0:T(8,128)(2,1)}, u32[]{:S(2)}) copy-start(bf16[8192,768]{1,0:T(8,128)(2,1)} %all-gather.10.cloned.1.call-done) | copy-start | bytes 37748740
  237.9 11.5 copy-start.22
  249.4 11.1 copy-start.40
  260.5 18.1 %copy-start.59 = (f32[8,3,256]{2,1,0:T(4,128)}, f32[8,3,256]{2,1,0:T(4,128)S(1)}, u32[]{:S(2)}) copy-start(f32[8,3,256]{2,1,0:T(4,128)S(1)} %fusion) | copy-start | bytes 73732
  283.3 88.5 %all-gather.16.cloned.1.call-start = ((), (), s32[]{:S(2)}) async-start(), calls=%async_computation.14 | async-start | bytes 3932160 | tf_op jit(solution)/shard_map/all_gather | solution.py:41
  283.9 118.6 %all-gather.14.cloned.1.call-start = ((), (), s32[]{:S(2)}) async-start(), calls=%async_computation.12 | async-start | bytes 3932160 | tf_op jit(solution)/shard_map/all_gather | solution.py:41
  345.7 133.3 %reduce-scatter.14.cloned.1.call-start = ((), (), s32[]{:S(2)}) async-start(), calls=%async_computation.15 | async-start | bytes 7864320 | tf_op jit(solution)/shard_map/reduce_scatter | solution.py:45
  420.5 61.6 %copy-start.76 = (f32[512]{0:T(512)S(1)}, f32[512]{0:T(512)}, u32[]{:S(2)}) copy-start(f32[512]{0:T(512)} %copy-done.75) | copy-start | bytes 6148
  420.5 61.6 %copy-start.17 = (bf16[512,768]{1,0:T(8,128)(2,1)S(1)}, bf16[512,768]{1,0:T(8,128)(2,1)}, u32[]{:S(2)}) copy-start(bf16[512,768]{1,0:T(8,128)(2,1)} %param.38) | copy-start | bytes 2359300
  420.5 93.1 %all-gather.18.cloned.1.call-start = ((), (), s32[]{:S(2)}) async-start(), calls=%async_computation.16 | async-start | bytes 3932160 | tf_op jit(solution)/shard_map/all_gather | solution.py:41
  482.1 31.6 %copy-start.43 = (bf16[192,768]{1,0:T(8,128)(2,1)S(1)}, bf16[192,768]{1,0:T(8,128)(2,1)}, u32[]{:S(2)}) copy-start(bf16[192,768]{1,0:T(8,128)(2,1)} %param.34) | copy-start | bytes 884740
  484.9 152.9 %reduce-scatter.16.cloned.1.call-start = ((), (), s32[]{:S(2)}) async-start(), calls=%async_computation.17 | async-start | bytes 7864320 | tf_op jit(solution)/shard_map/reduce_scatter | solution.py:45
  540.4 21.9 %copy-start.4 = (bf16[24,8,8,1024]{3,2,1,0:T(8,128)(2,1)S(1)}, bf16[24,8,8,1024]{3,2,1,0:T(8,128)(2,1)}, u32[]{:S(2)}) copy-start(bf16[24,8,8,1024]{3,2,1,0:T(8,128)(2,1)} %copy.165) | copy-start | bytes 9437188
  579.3 119.5 %reduce-scatter.12.cloned.1.call-start = ((), (), s32[]{:S(2)}) async-start(), calls=%async_computation.13 | async-start | bytes 7864320 | tf_op jit(solution)/shard_map/reduce_scatter | solution.py:45
  589.9 153.8 %all-gather.20.cloned.1.call-start = ((), (), s32[]{:S(2)}) async-start(), calls=%async_computation.18 | async-start | bytes 3932160 | tf_op jit(solution)/shard_map/all_gather | solution.py:41
  597.8 40.0 %copy-start.62 = (f32[768]{0:T(1024)S(1)}, f32[768]{0:T(1024)}, u32[]{:S(2)}) copy-start(f32[768]{0:T(1024)} %copy-done.61) | copy-start | bytes 9220
  597.8 40.0 %copy-start.68 = (f32[512]{0:T(512)S(1)}, f32[512]{0:T(512)}, u32[]{:S(2)}) copy-start(f32[512]{0:T(512)} %copy-done.67) | copy-start | bytes 6148
  605.1 35.1 %copy-start.70 = (f32[512]{0:T(512)S(1)}, f32[512]{0:T(512)}, u32[]{:S(2)}) copy-start(f32[512]{0:T(512)} %copy-done.69) | copy-start | bytes 6148
  605.1 93.6 %copy-start.72 = (f32[512]{0:T(512)S(1)}, f32[512]{0:T(512)}, u32[]{:S(2)}) copy-start(f32[512]{0:T(512)} %copy-done.71) | copy-start | bytes 6148
  704.3 241.0 %all-reduce.4.cloned.1.call-start = ((), (), s32[]{:S(2)}) async-start(), calls=%async_computation.21 | async-start | bytes 9437184 | tf_op jit(solution)/shard_map/psum | solution.py:269
  715.7 21.0 %slice-start.2 = ((s8[12582912]{0:T(1024)(128)(4,1)}), s8[4194304]{0:T(1024)(128)(4,1)S(1)}, s32[]{:S(2)}) async-start(s8[12582912]{0:T(1024)(128)(4,1)} %bitcast.222), calls=%async_computation.24 | async-start | bytes 8388608
  719.6 17.0 %copy-start.8 = (bf16[24,8,8,1024]{3,1,2,0:T(8,128)(2,1)}, bf16[24,8,8,1024]{3,1,2,0:T(8,128)(2,1)S(1)}, u32[]{:S(2)}) copy-start(bf16[24,8,8,1024]{3,1,2,0:T(8,128)(2,1)S(1)} %copy.174) | copy-start | bytes 9437188
  719.6 17.0 %slice-start.3 = ((s8[12582912]{0:T(1024)(128)(4,1)}), s8[4194304]{0:T(1024)(128)(4,1)S(1)}, s32[]{:S(2)}) async-start(s8[12582912]{0:T(1024)(128)(4,1)} %bitcast.222), calls=%async_computation.25 | async-start | bytes 8388608
  771.8 14.8 %copy-start.37 = (bf16[768,192]{0,1:T(8,128)(2,1)S(1)}, bf16[768,192]{0,1:T(8,128)(2,1)}, u32[]{:S(2)}) copy-start(bf16[768,192]{0,1:T(8,128)(2,1)} %param.33) | copy-start | bytes 884740
  771.8 274.1 %reduce-scatter.20.cloned.1.call-start = ((), (), s32[]{:S(2)}) async-start(), calls=%async_computation.20 | async-start | bytes 15728640 | tf_op jit(solution)/shard_map/reduce_scatter | solution.py:217
  801.3 305.5 %reduce-scatter.18.cloned.1.call-start = ((), (), s32[]{:S(2)}) async-start(), calls=%async_computation.19 | async-start | bytes 7864320 | tf_op jit(solution)/shard_map/reduce_scatter | solution.py:45
  945.4 9.2 copy-start.52
  945.4 10.1 copy-start.51
  959.5 147.3 %copy-start.10 = (bf16[512,768]{1,0:T(8,128)(2,1)S(1)}, bf16[512,768]{1,0:T(8,128)(2,1)}, u32[]{:S(2)}) copy-start(bf16[512,768]{1,0:T(8,128)(2,1)} %param.20) | copy-start | bytes 2359300
  959.5 147.3 %copy-start.64 = (f32[768]{0:T(1024)S(1)}, f32[768]{0:T(1024)}, u32[]{:S(2)}) copy-start(f32[768]{0:T(1024)} %copy-done.63) | copy-start | bytes 9220
  959.5 147.3 %copy-start.66 = (f32[512]{0:T(512)S(1)}, f32[512]{0:T(512)}, u32[]{:S(2)}) copy-start(f32[512]{0:T(512)} %copy-done.65) | copy-start | bytes 6148
  959.5 150.1 %copy-start.74 = (f32[512]{0:T(512)S(1)}, f32[512]{0:T(512)}, u32[]{:S(2)}) copy-start(f32[512]{0:T(512)} %copy-done.73) | copy-start | bytes 6148
  959.5 150.7 %copy-start.77 = (f32[768]{0:T(1024)S(1)}, f32[768]{0:T(1024)}, u32[]{:S(2)}) copy-start(f32[768]{0:T(1024)} %get-tuple-element.17) | copy-start | bytes 9220
  1106.8 43.1 %copy-start.24 = (f32[512,768]{1,0:T(8,128)S(1)}, f32[512,768]{1,0:T(8,128)}, u32[]{:S(2)}) copy-start(f32[512,768]{1,0:T(8,128)} %reduce-scatter.18.cloned.1.call-done) | copy-start | bytes 4718596
  1106.8 46.0 %copy-start.1 = (bf16[768,768]{1,0:T(8,128)(2,1)S(1)}, bf16[768,768]{1,0:T(8,128)(2,1)}, u32[]{:S(2)}) copy-start(bf16[768,768]{1,0:T(8,128)(2,1)} %param.36) | copy-start | bytes 3538948
  (59 other events, 166.4 us)
Sparse Core Ops, SparseCore 0:
  13.0 31.2 all-gather.7
  61.7 58.3 reduce-scatter.7
  121.7 82.0 all-gather.9
  205.9 28.5 all-gather.11
  283.4 58.3 reduce-scatter.9
  343.2 28.5 all-gather.15
  374.0 28.5 all-gather.13
  420.6 58.3 reduce-scatter.13
  485.1 28.5 all-gather.17
  579.4 58.3 reduce-scatter.15
  640.4 58.3 reduce-scatter.11
  704.5 28.5 all-gather.19
  771.9 173.4 all-reduce.3
  948.0 97.7 reduce-scatter.19
  1048.4 58.3 reduce-scatter.17
where the time goes:
time: 1170 us; the launch traced here: 1160 us
  waiting for transfers between devices  701 us (60%)
  matrix products  240 us (21%)
  other arithmetic  92 us (8%)
  blocking collectives  62.1 us (5%)
  local copies, waits for them, and re-layouts  48.1 us (4%)
  between operations  15.3 us (1%)
    reduce_scatter x6, waiting for transfers between devices, spread_rows(): return lax.psum_scatter(values, 'tensor', scatter_dimension=0, tiled=True)  321 us
    psum x1, waiting for transfers between devices, local(): lax.psum(grad_self_query.astype(jnp.bfloat16), 'dp').astype(jnp.float32)  109 us
    all_gather x6, waiting for transfers between devices, collect_rows(): return lax.all_gather(values, 'tensor', axis=0, tiled=True)  103 us
    reduce_scatter x1, waiting for transfers between devices, local(): lax.psum_scatter((times_transposed(grad_key, cross_key) + times_transpose...  86.4 us
    all_gather x1, waiting for transfers between devices, local(): enc_full = lax.all_gather(enc_states, 'tensor', axis=0, tiled=True)  80 us
    dot_general x10, matrix products, times_transposed(): lax.dot_general(former, latter, (((1,), (1,)), ((), ())), preferred_eleme...  56.5 us
    dot_general x10, matrix products, matmul(): return jnp.dot(former, latter, preferred_element_type=jnp.float32)  51.9 us
    psum x1, blocking collectives, local(): lax.psum((grad_gain_self, grad_gain_cross, grad_gain_ff), ('dp', 'tensor'))  39.7 us
  transfers between devices with their start and end apart: 15, of which 14 were waited for; matrix products, arithmetic and copies ran while one was open for 15% of the time, Pallas kernels for 0%

commit v1 on v0

--- a/solution.py
+++ b/solution.py
@@ -253,6 +253,7 @@
     )
     back_values, grad_gain_self = norm_back(residual, scale_self, spread_rows(grad_normed))
     grad_in = grad_after_self + back_values
+    load_cycles = lambda local_block, net_axis: lax.all_gather(local_block, net_axis).sum(axis=0)
     (
         grad_self_query,
         grad_self_key,
@@ -266,7 +267,7 @@
         grad_ff_in,
         grad_ff_out,
     ) = (
-        lax.psum(grad_self_query.astype(jnp.bfloat16), "dp").astype(jnp.float32),
+        load_cycles(grad_self_query.astype(jnp.bfloat16), "dp").astype(jnp.float32),
         lax.psum(grad_self_key.astype(jnp.bfloat16), "dp").astype(jnp.float32),
         lax.psum(grad_self_value.astype(jnp.bfloat16), "dp").astype(jnp.float32),
         lax.psum(grad_self_out.astype(jnp.bfloat16), "dp").astype(jnp.float32),

time: 1170 us -> 1200 us (1.026)
  waiting for transfers between devices: 701 us -> 725 us
    reduce_scatter x6, waiting for transfers between devices: 321 us -> 336 us  [spread_rows(): return lax.psum_scatter(values, 'tensor', scatter_dimension=0, tiled=True)]
    unnamed x200 -> x219, local copies, waits for them, and re-layouts: 28.9 us -> 31.6 us
  transfers between devices with their start and end apart: 15 -> 16, of which waited for: 14 -> 14; matrix products, arithmetic and copies ran while one was open for 15% -> 16% of each run, Pallas kernels for 0% -> 0%
where the time goes in v1:
time: 1200 us; the launch traced here: 1190 us
  waiting for transfers between devices  725 us (60%)
  matrix products  243 us (20%)
  other arithmetic  93.9 us (8%)
  blocking collectives  62.5 us (5%)
  local copies, waits for them, and re-layouts  52.6 us (4%)
  between operations  15.4 us (1%)
    reduce_scatter x6, waiting for transfers between devices, spread_rows(): return lax.psum_scatter(values, 'tensor', scatter_dimension=0, tiled=True)  336 us
    psum x1, waiting for transfers between devices, local(): lax.psum(grad_self_key.astype(jnp.bfloat16), 'dp').astype(jnp.float32)  117 us
    all_gather x6, waiting for transfers between devices, collect_rows(): return lax.all_gather(values, 'tensor', axis=0, tiled=True)  103 us
    reduce_scatter x1, waiting for transfers between devices, local(): lax.psum_scatter((times_transposed(grad_key, cross_key) + times_transpose...  87.3 us
    all_gather x1, waiting for transfers between devices, local(): enc_full = lax.all_gather(enc_states, 'tensor', axis=0, tiled=True)  80.1 us
    dot_general x10, matrix products, times_transposed(): lax.dot_general(former, latter, (((1,), (1,)), ((), ())), preferred_eleme...  56.1 us
    dot_general x10, matrix products, matmul(): return jnp.dot(former, latter, preferred_element_type=jnp.float32)  51.9 us
    psum x1, blocking collectives, local(): lax.psum((grad_gain_self, grad_gain_cross, grad_gain_ff), ('dp', 'tensor'))  39.7 us
  transfers between devices with their start and end apart: 16, of which 14 were waited for; matrix products, arithmetic and copies ran while one was open for 16% of the time, Pallas kernels for 0%

profile of v1, /device:TPU:0, one launch (start us, length us, event | category | flops | bytes accessed | tf_op | source)
XLA Modules:
  0.0 1194.2 jit_solution(7783508767220800190)
XLA Ops:
  14.8 11.5 copy.126
  28.8 15.5 %all-gather.10.cloned.1.call-done = bf16[2048,768]{1,0:T(8,128)(2,1)} async-done(((bf16[512,768]{1,0:T(8,128)(2,1)}), bf16[2048,768]{1,0:T(8,128)(2,1)}) %all-gather.10.cloned.1.call-update) | async-done | bytes 3145744 | tf_op jit(solution)/shard_map/all_gather | solution.py:41
  57.8 3.7 fusion.89
  62.4 57.7 %reduce-scatter.8.cloned.1.call-done = f32[512,768]{1,0:T(8,128)} async-done(((f32[2048,768]{1,0:T(8,128)}), f32[512,768]{1,0:T(8,128)}) %reduce-scatter.8.cloned.1.call-update) | async-done | bytes 1572880 | tf_op jit(solution)/shard_map/reduce_scatter | solution.py:45
  123.8 80.1 %all-gather.12.cloned.1.call-done = bf16[8192,768]{1,0:T(8,128)(2,1)} async-done(((bf16[2048,768]{1,0:T(8,128)(2,1)}), bf16[8192,768]{1,0:T(8,128)(2,1)}) %all-gather.12.cloned.1.call-update) | async-done | bytes 12582928 | tf_op jit(solution)/shard_map/all_gather | solution.py:180
  203.9 8.9 convolution_convert_fusion
  212.8 3.8 copy.165
  216.6 4.4 convolution_convert_fusion.1
  221.0 3.9 copy.163
  224.9 9.6 all-gather.14.cloned.1.call-done
  237.9 11.5 select_reduce_fusion
  249.5 11.0 fusion
  260.5 18.0 %fusion.58 = bf16[8,256,3,64]{1,3,2,0:T(8,128)(2,1)S(1)} fusion(f32[8,3,256,1024]{3,2,1,0:T(8,128)} %get-tuple-element.47, f32[8,3,256]{2,1,0:T(4,128)S(1)} %fusion, f32[8,3,256]{2,1,0:T(4,128)S(1)} %get-tuple-element.46, pred[8,1024]{1,0:T(8,128)(4,1)S(1)} %iota_compare_fusion.2, bf16[8,1024,3,64]{1,0,3,2:T(8,128)(2,1)} %bitcast.189), kind=kOutput, calls=%fused_computation.97 | convolution fusion | flops 830865408 | bytes 29155328 | tf_op jit(solution)/shard_map/shqk,skhd->sqhd/dot_general | solution.py:92
  279.5 3.7 fusion.90
  284.0 57.9 %reduce-scatter.10.cloned.1.call-done = f32[512,768]{1,0:T(8,128)} async-done(((f32[2048,768]{1,0:T(8,128)}), f32[512,768]{1,0:T(8,128)}) %reduce-scatter.10.cloned.1.call-update) | async-done | bytes 1572880 | tf_op jit(solution)/shard_map/reduce_scatter | solution.py:45
  345.8 26.0 %all-gather.18.cloned.1.call-done = bf16[2048,768]{1,0:T(8,128)(2,1)} async-done(((bf16[512,768]{1,0:T(8,128)(2,1)}), bf16[2048,768]{1,0:T(8,128)(2,1)}) %all-gather.18.cloned.1.call-update) | async-done | bytes 3145744 | tf_op jit(solution)/shard_map/all_gather | solution.py:41
  371.8 7.6 fusion.91
  379.4 23.1 %all-gather.16.cloned.1.call-done = bf16[2048,768]{1,0:T(8,128)(2,1)} async-done(((bf16[512,768]{1,0:T(8,128)(2,1)}), bf16[2048,768]{1,0:T(8,128)(2,1)}) %all-gather.16.cloned.1.call-update) | async-done | bytes 3145744 | tf_op jit(solution)/shard_map/all_gather | solution.py:41
  402.5 11.7 fusion.14
  415.9 4.5 fusion.92
  420.6 58.4 %reduce-scatter.14.cloned.1.call-done = f32[512,768]{1,0:T(8,128)} async-done(((f32[2048,768]{1,0:T(8,128)}), f32[512,768]{1,0:T(8,128)}) %reduce-scatter.14.cloned.1.call-update) | async-done | bytes 1572880 | tf_op jit(solution)/shard_map/reduce_scatter | solution.py:45
  485.0 28.6 %all-gather.20.cloned.1.call-done = bf16[2048,768]{1,0:T(8,128)(2,1)} async-done(((bf16[512,768]{1,0:T(8,128)(2,1)}), bf16[2048,768]{1,0:T(8,128)(2,1)}) %all-gather.20.cloned.1.call-update) | async-done | bytes 3145744 | tf_op jit(solution)/shard_map/all_gather | solution.py:41
  516.9 23.2 %multiply_reduce_fusion = (f32[8,3,256]{2,1,0:T(4,128)S(1)}, f32[8,3,256,1024]{3,2,1,0:T(8,128)}) fusion(f32[8,3,256,1024]{3,2,1,0:T(8,128)} %get-tuple-element.47, f32[8,3,256]{2,1,0:T(4,128)S(1)} %log_add_fusion.1, pred[8,1024]{1,0:T(8,128)(4,1)S(1)} %iota_compare_fusion.2, bf16[8,1024,3,64]{1,0,3,2:T(8,128)(2,1)} %bitcast.190, ...), kind=kOutput, calls=%fused_computation.2 | convolution fusion | flops 830466048 | bytes 54321152 | tf_op jit(solution)/shard_map/sqhd,skhd->shqk/dot_general | solution.py:111
  540.1 21.9 %multiply_convert_fusion = bf16[8,3,256,1024]{3,2,1,0:T(8,128)(2,1)} fusion(f32[8,3,256,1024]{3,2,1,0:T(8,128)} %get-tuple-element.51, f32[8,3,256,1024]{3,2,1,0:T(8,128)} %get-tuple-element.47, f32[8,3,256]{2,1,0:T(4,128)S(1)} %get-tuple-element.50, f32[8,3,256]{2,1,0:T(4,128)S(1)} %log_add_fusion.1, pred[8,1024]{1,0:T(8,128)(4,1)S(1)} %iota_compare_fusion.2), kind=kLoop, calls=%fused_computation.1 | loop fusion | flops 31457280 | bytes 62971904 | tf_op jit(solution)/shard_map/convert_element_type | solution.py:115
  562.0 10.4 fusion.53
  575.1 3.7 fusion.93
  578.9 10.6 fusion.85
  589.6 47.8 %reduce-scatter.16.cloned.1.call-done = f32[512,768]{1,0:T(8,128)} async-done(((f32[2048,768]{1,0:T(8,128)}), f32[512,768]{1,0:T(8,128)}) %reduce-scatter.16.cloned.1.call-update) | async-done | bytes 1572880 | tf_op jit(solution)/shard_map/reduce_scatter | solution.py:45
  639.9 58.5 %reduce-scatter.12.cloned.1.call-done = f32[512,768]{1,0:T(8,128)} async-done(((f32[2048,768]{1,0:T(8,128)}), f32[512,768]{1,0:T(8,128)}) %reduce-scatter.12.cloned.1.call-update) | async-done | bytes 1572880 | tf_op jit(solution)/shard_map/reduce_scatter | solution.py:45
  698.3 5.6 fusion.86
  704.4 6.7 convolution_convert_fusion.9
  711.1 7.8 convolution_convert_fusion.8
  718.9 3.9 convert_bitcast_fusion.1
  722.8 12.5 %convert_bitcast_fusion = bf16[8,1024,3,64]{1,3,2,0:T(8,128)(2,1)} fusion(f32[8,3,256,1024]{3,2,1,0:T(8,128)} %get-tuple-element.47, f32[8,3,256]{2,1,0:T(4,128)S(1)} %log_add_fusion.1, pred[8,1024]{1,0:T(8,128)(4,1)S(1)} %iota_compare_fusion.2, bf16[8,256,3,64]{1,0,3,2:T(8,128)(2,1)S(1)} %bitcast.194), kind=kOutput, calls=%fused_computation.39 | convolution fusion | flops 825753600 | bytes 29130752 | tf_op jit(solution)/shard_map/shqk,sqhd->skhd/dot_general | solution.py:105
  738.7 7.3 multiply_reduce_fusion.1
  746.1 5.6 convert_reduce_fusion
  771.7 8.1 fusion.62
  779.8 3.9 fusion.61
  794.3 13.8 %fusion.96 = f32[8192,768]{1,0:T(8,128)} fusion(bf16[8192,192]{0,1:T(8,128)(2,1)} %bitcast.188, bf16[768,192]{0,1:T(8,128)(2,1)S(1)} %copy-done.40), kind=kOutput, calls=%fused_computation.155 | convolution fusion | flops 2415919104 | bytes 28606464 | tf_op jit(solution)/shard_map/dot_general | solution.py:77
  808.1 14.5 %add_convert_fusion = bf16[8192,768]{1,0:T(8,128)(2,1)} fusion(f32[8192,768]{1,0:T(8,128)} %fusion.96, bf16[8192,192]{0,1:T(8,128)(2,1)} %bitcast.186, bf16[768,192]{0,1:T(8,128)(2,1)S(1)} %copy-done.42), kind=kOutput, calls=%fused_computation | convolution fusion | flops 2428502016 | bytes 41189376 | tf_op jit(solution)/shard_map/dot_general | solution.py:77
  825.7 3.8 add_add_fusion
  830.7 4.1 fusion.63
  834.8 22.8 %psum.95 = bf16[32,3]{0,1:T(4,128)(2,1)S(1)} all-reduce(bf16[32,3]{0,1:T(4,128)(2,1)S(1)} %fusion.63), channel_id=1, replica_groups=mesh['dp'=8,'tensor'=4] {'dp'}, use_global_device_ids=true, to_apply=%region_27.28 | all-reduce | flops 96 | bytes 384 | tf_op jit(solution)/shard_map/psum | solution.py:274
  863.0 117.0 %all-reduce.4.cloned.1.call-done = (bf16[768,192]{0,1:T(8,128)(2,1)}, bf16[768,192]{0,1:T(8,128)(2,1)}, bf16[192,768]{1,0:T(8,128)(2,1)}, bf16[768,192]{0,1:T(8,...) async-done(((bf16[768,192]{0,1:T(8,128)(2,1)}, ...) | async-done | bytes 4423696 | tf_op jit(solution)/shard_map/psum | solution.py:271
  993.2 87.3 %reduce-scatter.20.cloned.1.call-done = bf16[2048,768]{1,0:T(8,128)(2,1)} async-done(((bf16[8192,768]{1,0:T(8,128)(2,1)}), bf16[2048,768]{1,0:T(8,128)(2,1)}) %reduce-scatter.20.cloned.1.call-update) | async-done | bytes 3145744 | tf_op jit(solution)/shard_map/reduce_scatter | solution.py:217
  1080.5 5.1 convert_element_type.262
  1085.5 55.9 %reduce-scatter.18.cloned.1.call-done = f32[512,768]{1,0:T(8,128)} async-done(((f32[2048,768]{1,0:T(8,128)}), f32[512,768]{1,0:T(8,128)}) %reduce-scatter.18.cloned.1.call-update) | async-done | bytes 1572880 | tf_op jit(solution)/shard_map/reduce_scatter | solution.py:45
  1144.8 39.7 %all-reduce = (f32[768]{0:T(1024)}, f32[768]{0:T(1024)}, f32[768]{0:T(1024)}) all-reduce(f32[768]{0:T(1024)} %get-tuple-element.21, f32[768]{0:T(1024)} %get-tuple-element.19, f32[768]{0:T(1024)S(1)} %copy-done.81), channel_id=1, replica_groups=mesh['dp'=8,'tensor'=4] {'dp','tensor'}, use_global_device_ids=true, to_apply=%region_21.22 | all-reduce | flops 2304 | bytes 18432 | tf_op jit(solution)/shard_map/psum | solution.py:282
  (328 shorter events, 116.2 us)
Async XLA Ops:
  7.2 395.3 %copy-start = (bf16[768,768]{1,0:T(8,128)(2,1)S(1)}, bf16[768,768]{1,0:T(8,128)(2,1)}, u32[]{:S(2)}) copy-start(bf16[768,768]{1,0:T(8,128)(2,1)} %param.36) | copy-start | bytes 3538948
  7.2 37.0 %all-gather.10.cloned.1.call-start = ((), (), s32[]{:S(2)}) async-start(), calls=%async_computation.7 | async-start | bytes 3932160 | tf_op jit(solution)/shard_map/all_gather | solution.py:41
  12.9 107.2 %reduce-scatter.8.cloned.1.call-start = ((), (), s32[]{:S(2)}) async-start(), calls=%async_computation.8 | async-start | bytes 7864320 | tf_op jit(solution)/shard_map/reduce_scatter | solution.py:45
  13.6 12.7 %copy-start.84 = (bf16[32,3]{0,1:T(4,128)(2,1)S(1)}, bf16[32,3]{0,1:T(4,128)(2,1)}, u32[]{:S(2)}) copy-start(bf16[32,3]{0,1:T(4,128)(2,1)} %param.29) | copy-start | bytes 580
  26.3 17.9 %copy-start.54 = (bf16[768,192]{0,1:T(8,128)(2,1)S(1)}, bf16[768,192]{0,1:T(8,128)(2,1)}, u32[]{:S(2)}) copy-start(bf16[768,192]{0,1:T(8,128)(2,1)} %param.26) | copy-start | bytes 884740
  28.8 18.9 %copy-start.52 = (bf16[768,192]{0,1:T(8,128)(2,1)S(1)}, bf16[768,192]{0,1:T(8,128)(2,1)}, u32[]{:S(2)}) copy-start(bf16[768,192]{0,1:T(8,128)(2,1)} %param.25) | copy-start | bytes 884740
  61.6 58.5 %copy-start.12 = (bf16[512,768]{1,0:T(8,128)(2,1)S(1)}, bf16[512,768]{1,0:T(8,128)(2,1)}, u32[]{:S(2)}) copy-start(bf16[512,768]{1,0:T(8,128)(2,1)} %param.20) | copy-start | bytes 2359300
  61.6 142.3 %all-gather.12.cloned.1.call-start = ((), (), s32[]{:S(2)}) async-start(), calls=%async_computation.9 | async-start | bytes 15728640 | tf_op jit(solution)/shard_map/all_gather | solution.py:180
  62.3 172.2 %all-gather.14.cloned.1.call-start = ((), (), s32[]{:S(2)}) async-start(), calls=%async_computation.10 | async-start | bytes 3932160 | tf_op jit(solution)/shard_map/all_gather | solution.py:41
  62.4 61.0 %copy-start.65 = (f32[768]{0:T(1024)}, f32[768]{0:T(1024)S(1)}, u32[]{:S(2)}) copy-start(f32[768]{0:T(1024)S(1)} %convert_element_type.228) | copy-start | bytes 9220
  62.4 61.3 %copy-start.87 = (s32[8]{0:T(128)S(1)}, s32[8]{0:T(128)}, u32[]{:S(2)}) copy-start(s32[8]{0:T(128)} %param.23) | copy-start | bytes 100
  122.3 90.4 %copy-start.71 = (f32[512]{0:T(512)}, f32[512]{0:T(512)S(1)}, u32[]{:S(2)}) copy-start(f32[512]{0:T(512)S(1)} %fusion.79) | copy-start | bytes 6148
  123.5 218.4 %reduce-scatter.10.cloned.1.call-start = ((), (), s32[]{:S(2)}) async-start(), calls=%async_computation.11 | async-start | bytes 7864320 | tf_op jit(solution)/shard_map/reduce_scatter | solution.py:45
  203.9 12.8 %copy-start.88 = (bf16[8192,768]{1,0:T(8,128)(2,1)S(1)}, bf16[8192,768]{1,0:T(8,128)(2,1)}, u32[]{:S(2)}) copy-start(bf16[8192,768]{1,0:T(8,128)(2,1)} %all-gather.12.cloned.1.call-done) | copy-start | bytes 37748740
  260.5 18.1 %copy-start.63 = (f32[8,3,256]{2,1,0:T(4,128)}, f32[8,3,256]{2,1,0:T(4,128)S(1)}, u32[]{:S(2)}) copy-start(f32[8,3,256]{2,1,0:T(4,128)S(1)} %fusion) | copy-start | bytes 73732
  283.3 88.5 %all-gather.18.cloned.1.call-start = ((), (), s32[]{:S(2)}) async-start(), calls=%async_computation.14 | async-start | bytes 3932160 | tf_op jit(solution)/shard_map/all_gather | solution.py:41
  283.9 118.6 %all-gather.16.cloned.1.call-start = ((), (), s32[]{:S(2)}) async-start(), calls=%async_computation.12 | async-start | bytes 3932160 | tf_op jit(solution)/shard_map/all_gather | solution.py:41
  345.8 133.2 %reduce-scatter.14.cloned.1.call-start = ((), (), s32[]{:S(2)}) async-start(), calls=%async_computation.15 | async-start | bytes 7864320 | tf_op jit(solution)/shard_map/reduce_scatter | solution.py:45
  420.5 61.6 %copy-start.80 = (f32[512]{0:T(512)S(1)}, f32[512]{0:T(512)}, u32[]{:S(2)}) copy-start(f32[512]{0:T(512)} %copy-done.79) | copy-start | bytes 6148
  420.5 61.6 %copy-start.21 = (bf16[512,768]{1,0:T(8,128)(2,1)S(1)}, bf16[512,768]{1,0:T(8,128)(2,1)}, u32[]{:S(2)}) copy-start(bf16[512,768]{1,0:T(8,128)(2,1)} %param.38) | copy-start | bytes 2359300
  420.5 93.1 %all-gather.20.cloned.1.call-start = ((), (), s32[]{:S(2)}) async-start(), calls=%async_computation.16 | async-start | bytes 3932160 | tf_op jit(solution)/shard_map/all_gather | solution.py:41
  482.0 31.6 %copy-start.48 = (bf16[192,768]{1,0:T(8,128)(2,1)S(1)}, bf16[192,768]{1,0:T(8,128)(2,1)}, u32[]{:S(2)}) copy-start(bf16[192,768]{1,0:T(8,128)(2,1)} %param.34) | copy-start | bytes 884740
  484.9 152.5 %reduce-scatter.16.cloned.1.call-start = ((), (), s32[]{:S(2)}) async-start(), calls=%async_computation.17 | async-start | bytes 7864320 | tf_op jit(solution)/shard_map/reduce_scatter | solution.py:45
  540.1 21.9 %copy-start.4 = (bf16[24,8,8,1024]{3,2,1,0:T(8,128)(2,1)S(1)}, bf16[24,8,8,1024]{3,2,1,0:T(8,128)(2,1)}, u32[]{:S(2)}) copy-start(bf16[24,8,8,1024]{3,2,1,0:T(8,128)(2,1)} %copy.165) | copy-start | bytes 9437188
  578.9 119.5 %reduce-scatter.12.cloned.1.call-start = ((), (), s32[]{:S(2)}) async-start(), calls=%async_computation.13 | async-start | bytes 7864320 | tf_op jit(solution)/shard_map/reduce_scatter | solution.py:45
  589.5 47.9 %copy-start.66 = (f32[768]{0:T(1024)S(1)}, f32[768]{0:T(1024)}, u32[]{:S(2)}) copy-start(f32[768]{0:T(1024)} %copy-done.65) | copy-start | bytes 9220
  589.5 47.9 %copy-start.72 = (f32[512]{0:T(512)S(1)}, f32[512]{0:T(512)}, u32[]{:S(2)}) copy-start(f32[512]{0:T(512)} %copy-done.71) | copy-start | bytes 6148
  589.5 50.3 %copy-start.74 = (f32[512]{0:T(512)S(1)}, f32[512]{0:T(512)}, u32[]{:S(2)}) copy-start(f32[512]{0:T(512)} %copy-done.73) | copy-start | bytes 6148
  589.5 108.8 %copy-start.76 = (f32[512]{0:T(512)S(1)}, f32[512]{0:T(512)}, u32[]{:S(2)}) copy-start(f32[512]{0:T(512)} %copy-done.75) | copy-start | bytes 6148
  589.5 145.8 %all-gather.22.cloned.1.call-start = ((), (), s32[]{:S(2)}) async-start(), calls=%async_computation.18 | async-start | bytes 3932160 | tf_op jit(solution)/shard_map/all_gather | solution.py:41
  639.8 64.5 %copy-start.44 = (f32[8,3,256]{2,1,0:T(4,128)S(1)}, f32[8,3,256]{2,1,0:T(4,128)}, u32[]{:S(2)}) copy-start(f32[8,3,256]{2,1,0:T(4,128)} %copy-done.43) | copy-start | bytes 73732
  639.8 64.5 %copy-start.62 = (f32[8,3,256]{2,1,0:T(4,128)S(1)}, f32[8,3,256]{2,1,0:T(4,128)}, u32[]{:S(2)}) copy-start(f32[8,3,256]{2,1,0:T(4,128)} %copy-done.61) | copy-start | bytes 73732
  703.9 154.3 %all-gather.24.cloned.1.call-start = ((), (), s32[]{:S(2)}) async-start(), calls=%async_computation.21 | async-start | bytes 2654208 | tf_op jit(solution)/shard_map/all_gather | solution.py:256
  704.4 14.5 %slice-start = ((s8[12582912]{0:T(1024)(128)(4,1)}), s8[4194304]{0:T(1024)(128)(4,1)S(1)}, s32[]{:S(2)}) async-start(s8[12582912]{0:T(1024)(128)(4,1)} %bitcast.177), calls=%async_computation.23 | async-start | bytes 8388608
  722.8 12.5 %copy-start.51 = (bf16[192,768]{1,0:T(8,128)(2,1)S(1)}, bf16[192,768]{1,0:T(8,128)(2,1)}, u32[]{:S(2)}) copy-start(bf16[192,768]{1,0:T(8,128)(2,1)} %param.28) | copy-start | bytes 884740
  756.3 223.7 %all-reduce.4.cloned.1.call-start = ((), (), s32[]{:S(2)}) async-start(), calls=%async_computation.22 | async-start | bytes 8847360 | tf_op jit(solution)/shard_map/psum | solution.py:271
  767.6 12.2 %slice-start.7 = ((s8[12582912]{0:T(1024)(128)(4,1)}), s8[4194304]{0:T(1024)(128)(4,1)S(1)}, s32[]{:S(2)}) async-start(s8[12582912]{0:T(1024)(128)(4,1)} %bitcast.232), calls=%async_computation.30 | async-start | bytes 8388608
  771.7 12.0 %slice-start.5 = ((s8[6291456]{0:T(1024)(128)(4,1)}), s8[4194304]{0:T(1024)(128)(4,1)S(1)}, s32[]{:S(2)}) async-start(s8[6291456]{0:T(1024)(128)(4,1)} %bitcast.181), calls=%async_computation.28 | async-start | bytes 8388608
  793.4 14.7 %copy-start.42 = (bf16[768,192]{0,1:T(8,128)(2,1)S(1)}, bf16[768,192]{0,1:T(8,128)(2,1)}, u32[]{:S(2)}) copy-start(bf16[768,192]{0,1:T(8,128)(2,1)} %param.33) | copy-start | bytes 884740
  793.4 287.1 %reduce-scatter.20.cloned.1.call-start = ((), (), s32[]{:S(2)}) async-start(), calls=%async_computation.20 | async-start | bytes 15728640 | tf_op jit(solution)/shard_map/reduce_scatter | solution.py:217
  822.6 318.8 %reduce-scatter.18.cloned.1.call-start = ((), (), s32[]{:S(2)}) async-start(), calls=%async_computation.19 | async-start | bytes 7864320 | tf_op jit(solution)/shard_map/reduce_scatter | solution.py:45
  993.2 148.3 %copy-start.13 = (bf16[512,768]{1,0:T(8,128)(2,1)S(1)}, bf16[512,768]{1,0:T(8,128)(2,1)}, u32[]{:S(2)}) copy-start(bf16[512,768]{1,0:T(8,128)(2,1)} %param.20) | copy-start | bytes 2359300
  993.2 148.3 %copy-start.68 = (f32[768]{0:T(1024)S(1)}, f32[768]{0:T(1024)}, u32[]{:S(2)}) copy-start(f32[768]{0:T(1024)} %copy-done.67) | copy-start | bytes 9220
  993.2 148.3 %copy-start.70 = (f32[512]{0:T(512)S(1)}, f32[512]{0:T(512)}, u32[]{:S(2)}) copy-start(f32[512]{0:T(512)} %copy-done.69) | copy-start | bytes 6148
  993.2 151.0 %copy-start.78 = (f32[512]{0:T(512)S(1)}, f32[512]{0:T(512)}, u32[]{:S(2)}) copy-start(f32[512]{0:T(512)} %copy-done.77) | copy-start | bytes 6148
  993.2 151.6 %copy-start.81 = (f32[768]{0:T(1024)S(1)}, f32[768]{0:T(1024)}, u32[]{:S(2)}) copy-start(f32[768]{0:T(1024)} %get-tuple-element.17) | copy-start | bytes 9220
  1141.4 43.1 %copy-start.30 = (f32[512,768]{1,0:T(8,128)S(1)}, f32[512,768]{1,0:T(8,128)}, u32[]{:S(2)}) copy-start(f32[512,768]{1,0:T(8,128)} %reduce-scatter.18.cloned.1.call-done) | copy-start | bytes 4718596
  1141.4 46.0 %copy-start.1 = (bf16[768,768]{1,0:T(8,128)(2,1)S(1)}, bf16[768,768]{1,0:T(8,128)(2,1)}, u32[]{:S(2)}) copy-start(bf16[768,768]{1,0:T(8,128)(2,1)} %param.36) | copy-start | bytes 3538948
  (69 other events, 252.9 us)
Sparse Core Ops, SparseCore 0:
  13.0 31.2 all-gather.9
  61.7 58.3 reduce-scatter.7
  121.7 82.0 all-gather.11
  205.9 28.5 all-gather.13
  283.4 58.3 reduce-scatter.9
  343.3 28.5 all-gather.17
  374.0 28.5 all-gather.15
  420.6 58.3 reduce-scatter.13
  485.0 28.5 all-gather.19
  579.0 58.3 reduce-scatter.15
  639.9 58.3 reduce-scatter.11
  704.0 28.5 all-gather.21
  756.4 52.2 all-gather.23
  815.8 164.1 all-reduce.3
  982.6 97.7 reduce-scatter.19
  1083.0 58.3 reduce-scatter.17
